TPU v7x, 32 devices: a whole 2x2x4 slice. The times are simulated.
32 devices in a mesh: tile: 8 (over y, x, core), mode: 4 (over z).
Axes of the slice: x: 2, y: 2, z: 4, core: 2. Of those that a mesh axis runs over, the one named last changes fastest.
Arguments:
- object_field: float32 [2, 2, 2048, 384], P(None, None, 'tile'), may hold values from -4 to 4
- probe: float32 [8, 2, 256, 256], P('mode'), may hold values from -4 to 4
- measured: float32 [32, 256, 256], P('tile'), may hold values from 0 to 16
- prop_phase: float32 [256, 256], replicated, may hold values from -3.140625 to 3.140625
- counts: int32 [8], P('tile'), may hold values from 1 to 4, 16 in all
- row_offset: int32 [32], P('tile'), may hold values from 0 to 255
- col_offset: int32 [32], P('tile'), may hold values from 0 to 128
Outputs:
- object_grad: float32 [2, 2, 2048, 384], P(None, None, 'tile')
- probe_grad: float32 [8, 2, 256, 256], P('mode')
Inputs may be any that keep to these rules, and one draw needn't show every extreme that they name: Slot i is live for i % 4 < counts[i // 4]; some tile has all 4 slots live.
All inputs are finite; a program needn't handle non-finite values. No bound on the sum of `counts` on one device may be relied on, other than what follows from the above.
Results may differ from a plain program's by a relative error of at most 0.0003.
Values sent between devices are 32-bit elements; how exact they have to be, the bound alone decides.
A program may use at most 128 MiB of HBM per device.

v0:
```python
import math
import jax
import jax.numpy as jnp
from jax import lax
from jax.sharding import PartitionSpec as P

MODES = 8
HIGH = lax.Precision.HIGHEST


def shifted(block, axis, distance):
    devices = range(lax.axis_size(axis))
    route = [(i - distance, i) for i in devices if i - distance in devices]
    return lax.ppermute(block, axis, route)


def dft_tables(length):
    indices = jnp.arange(length, dtype=jnp.int32)
    product = indices[:, None] * indices[None, :] % length
    angle = product.astype(jnp.float32) * (2.0 * math.pi / length)
    factor = 1.0 / math.sqrt(length)
    return (jnp.cos(angle) * factor, jnp.sin(angle) * factor)


def on_left(matrix, field):
    return jnp.einsum("jk,mkl->mjl", matrix, field, precision=HIGH)


def on_right(field, matrix):
    return jnp.einsum("mjk,kl->mjl", field, matrix, precision=HIGH)


def transform(pair, tables, sign):
    cosine, sine = tables
    real_in, imag_in = pair
    mid_real = on_left(cosine, real_in) - sign * on_left(sine, imag_in)
    mid_imag = on_left(cosine, imag_in) + sign * on_left(sine, real_in)
    out_real = on_right(mid_real, cosine) - sign * on_right(mid_imag, sine)
    out_imag = on_right(mid_imag, cosine) + sign * on_right(mid_real, sine)
    return (out_real, out_imag)


def times(first, second):
    return (
        first[0] * second[0] - first[1] * second[1],
        first[0] * second[1] + first[1] * second[0],
    )


def times_conj(first, second):
    return (
        first[0] * second[0] + first[1] * second[1],
        first[0] * second[1] - first[1] * second[0],
    )


def forward_pass(window, probe_pair, kernel, tables):
    wave = times(probe_pair, (window[0, 0], window[0, 1]))
    spectrum = transform(wave, tables, -1.0)
    moved = transform(times(kernel, spectrum), tables, 1.0)
    before = [moved]
    wave = times(moved, (window[1, 0], window[1, 1]))
    far_field = transform(wave, tables, -1.0)
    return (before, far_field)


def backward_pass(window, before, far_field, weight, probe_pair, kernel, tables):
    layers = window.shape[0]
    back = transform((weight * far_field[0], weight * far_field[1]), tables, 1.0)
    pieces = [None] * layers
    term = times_conj(before[0], back)
    pieces[1] = jnp.stack([jnp.sum(term[0], axis=0), jnp.sum(term[1], axis=0)])
    inner = transform(times_conj((window[1, 0], window[1, 1]), back), tables, -1.0)
    back = transform(times_conj(kernel, inner), tables, 1.0)
    first = times_conj(probe_pair, back)
    pieces[0] = jnp.stack([jnp.sum(first[0], axis=0), jnp.sum(first[1], axis=0)])
    probe_term = times_conj((window[0, 0], window[0, 1]), back)
    return (jnp.stack(pieces), jnp.stack([probe_term[0], probe_term[1]], axis=1))


def per_device(object_field, probe, measured, prop_phase, counts, row_offset, col_offset):
    layers, _, tile_rows, columns = object_field.shape
    width = probe.shape[-1]
    next_rows = shifted(object_field, "tile", -1)
    extended = jnp.concatenate([object_field, next_rows], axis=2)
    tables = dft_tables(width)
    kernel = (jnp.cos(prop_phase), jnp.sin(prop_phase))
    probe_pair = (probe[:, 0], probe[:, 1])
    live_count = counts[0]
    zero_index = jnp.zeros((), jnp.int32)
    slot_total = row_offset.shape[0]

    def cut_window(row_start, col_start):
        start = (zero_index, zero_index, row_start, col_start)
        return lax.dynamic_slice(extended, start, (layers, 2, width, width))

    def place_terms(grad_ext, pieces, row_start, col_start):
        start = (zero_index, zero_index, row_start, col_start)
        current = lax.dynamic_slice(grad_ext, start, (layers, 2, width, width))
        return lax.dynamic_update_slice(grad_ext, current + pieces, start)

    init = (jnp.zeros(extended.shape, jnp.float32), jnp.zeros(probe.shape, jnp.float32))
    windows = jax.vmap(cut_window)(row_offset, col_offset)
    before, far_field = jax.vmap(lambda item: forward_pass(item, probe_pair, kernel, tables))(
        windows
    )
    local_power = jnp.sum(far_field[0] * far_field[0] + far_field[1] * far_field[1], axis=1)
    power = lax.psum(local_power, "mode")
    alive = (jnp.arange(slot_total, dtype=jnp.int32) < live_count).astype(jnp.float32)
    weight = (power - measured) / MODES * alive[:, None, None]

    def one_back(item, item_before, item_far, item_weight):
        return backward_pass(item, item_before, item_far, item_weight, probe_pair, kernel, tables)

    all_pieces, probe_terms = jax.vmap(one_back)(windows, before, far_field, weight)
    grad_probe = jnp.sum(probe_terms, axis=0)

    def add_slot(slot, grad_ext):
        return place_terms(grad_ext, all_pieces[slot], row_offset[slot], col_offset[slot])

    grad_ext = lax.fori_loop(zero_index, jnp.full((), slot_total, jnp.int32), add_slot, init[0])
    summed = lax.psum(grad_ext, "mode")
    arrived = shifted(summed[:, :, tile_rows:, :], "tile", 1)
    object_grad = summed[:, :, :tile_rows, :].at[:, :, :width, :].add(arrived)
    probe_grad = lax.psum(grad_probe, "tile")
    return (object_grad, probe_grad)


def solution(mesh):
    placed = (
        P(None, None, "tile", None),
        P("mode", None, None, None),
        P("tile", None, None),
        P(),
        P("tile"),
        P("tile"),
        P("tile"),
    )
    return jax.shard_map(
        per_device,
        mesh=mesh,
        in_specs=placed,
        out_specs=(P(None, None, "tile", None), P("mode", None, None, None)),
        check_vma=False,
    )
```

profile of v0, /device:TPU:0, one launch (start us, length us, event | category | flops | bytes accessed | tf_op | source)
XLA Modules:
  0.0 612.1 jit_solution(3632968894506634922)
XLA Ops:
  10.1 2.6 fusion.421
  16.6 12.5 %while.14 = (s32[]{:T(128)}, f32[2,2,512,384]{3,2,1,0:T(8,128)S(1)}, s32[4,4]{1,0:T(4,128)S(1)}, f32[4,2,2,256,256]{4,3,2,1,0:T(8,128)}, s32[]{:T(128)}) while((s32[]{:T(128)}, f32[2,2,512,384]{3,2,1,0:T(8,128)S(1)}, s32[4,4]{1,0:T(4,128)S(1)}, f32[4,2,2,256,256]{4,3,2,1,0:T(8,128)}, s32[]{:T(128)}) %tuple.57), condition=%wide.while_cond.1, body=%wide.while_body.1.sunk | while | flops 2 | bytes 2098801 | solution.py:95
  20.4 2.5 bitcast_dynamic-update-slice_fusion.2
  26.6 2.5 bitcast_dynamic-update-slice_fusion.2
  29.2 2.7 slice_bitcast_fusion.3
  31.9 4.5 fusion.49
  36.4 4.4 fusion.48
  40.8 4.6 multiply_add_fusion.9
  45.4 4.3 fusion.40
  49.8 4.3 fusion.42
  54.1 4.7 multiply_subtract_fusion.9
  58.8 4.5 multiply_add_fusion.8
  63.2 4.8 multiply_subtract_fusion.8
  68.1 4.6 fusion.116
  72.7 4.6 fusion.117
  77.3 4.8 convolution_add_fusion.1
  82.1 4.5 fusion.34
  86.6 4.5 fusion.32
  91.0 4.8 convolution_subtract_fusion.1
  95.9 4.5 fusion.70
  100.3 4.5 fusion.73
  104.8 5.0 fusion.165
  109.9 4.6 fusion.162
  114.5 4.8 multiply_add_fusion.5
  119.3 4.5 fusion.26
  123.8 4.5 fusion.24
  128.3 4.8 multiply_subtract_fusion.5
  133.1 4.5 multiply_subtract_fusion.4
  137.6 7.2 %add_reduce_fusion.2 = (f32[4,256,256]{2,1,0:T(8,128)}, f32[4,2,256,256]{3,2,1,0:T(8,128)}) fusion(f32[4,2,256,256]{3,2,1,0:T(8,128)S(1)} %multiply_subtract_fusion.4, f32[4,2,256,256]{3,2,1,0:T(8,128)S(1)} %fusion.24, f32[4,2,256,256]{3,2,1,0:T(8,128)S(1)} %multiply_subtract_fusion.5), kind=kOutput, calls=%fused_computation.70 | convolution fusion | flops 1614479360 | bytes 9437184 | tf_op jit(solution)/shard_map/vmap(mjk,kl->mjl)/dot_general | solution.py:30
  145.9 67.4 %all-reduce.4.cloned.1.call-done = f32[4,256,256]{2,1,0:T(8,128)} async-done(((f32[4,256,256]{2,1,0:T(8,128)}), f32[4,256,256]{2,1,0:T(8,128)}) %all-reduce.4.cloned.1.call-update) | async-done | bytes 1048592 | tf_op jit(solution)/shard_map/psum | solution.py:108
  215.5 4.5 fusion.54
  220.0 4.5 fusion.52
  224.5 4.7 fusion.63
  229.2 4.6 fusion.18
  233.8 4.6 fusion.16
  238.3 4.7 fusion.60
  243.1 4.5 fusion.80
  247.6 5.6 add_reduce_fusion
  253.2 4.6 fusion.155
  257.8 4.6 fusion.152
  262.5 4.8 multiply_add_fusion.2
  267.3 4.5 fusion.8
  271.8 4.5 fusion.10
  276.3 4.9 multiply_subtract_fusion.2
  281.2 4.6 multiply_add_fusion.1
  285.8 4.6 multiply_subtract_fusion.1
  290.4 5.0 fusion.118
  295.4 4.6 fusion.119
  300.0 4.8 convolution_add_fusion
  304.8 4.5 fusion.2
  309.3 4.5 fusion
  313.8 4.9 convolution_subtract_fusion
  318.7 4.5 fusion.90
  323.2 7.6 %add_bitcast_fusion = (f32[4,2,1,256,256]{4,3,1,0,2:T(8,128)S(1)}, f32[4,2,1,256,256]{4,3,1,0,2:T(8,128)}, f32[4,256,256]{2,1,0:T(8,128)S(1)}, f32[4,256,256]{2,1,0:T(8,128)S(1)}) fusion(f32[4,2,256,256]{3,2,1,0:T(8,128)S(1)} %fusion.90, f32[4,256,256]{2,1,0:T(8,128)S(1)} %get-tuple-element.89, f32[4,256,256]{2,1,0:T(8,128)S(1)} %copy-done.5, ...), kind=kOutput, calls=%fused_computation.57 | convolution fusion | flops 1618935808 | bytes 15728640 | tf_op jit(solution)/shard_map/vmap(mjk,kl->mjl)/dot_general | solution.py:30
  335.3 75.1 %while.13 = (s32[]{:T(128)}, f32[2,2,512,384]{3,2,1,0:T(8,128)}, s32[4]{0:T(128)S(1)}, s32[4]{0:T(128)S(1)}, f32[4,2,2,256,256]{4,3,2,1,0:T(8,128)}, /*index=5*/s32[]{:T(128)}, s32[]{:T(128)}, s32[]{:T(128)}, s32[]{:T(128)}) while((s32[]{:T(128)}, f32[2,2,512,384]{3,2,1,0:T(8,128)}, s32[4]{0:T(128)S(1)}, s32[4]{0:T(128)S(1)}, ...), condition=%wide.region_7.8_spmd, body=%wide.region_6.7_spmd.sunk | while | flops 262152 | bytes 5243081 | solution.py:121
  342.4 11.9 %dynamic_update_slice.4 = f32[2,2,512,384]{3,2,1,0:T(8,128)} dynamic-update-slice(f32[2,2,512,384]{3,2,1,0:T(8,128)} %get-tuple-element.186, f32[2,2,256,256]{3,2,1,0:T(8,128)S(1)} %bitcast_add_fusion.2, s32[]{:T(128)} %constant.72.clone.1..sunk, s32[]{:T(128)} %constant.72.clone.1..sunk, s32[]{:T(128)S(6)} %select_n.288, s32[]{:T(128)S(6)} %select_n.289) | dynamic-update-slice | bytes 2097156 | tf_op jit(solution)/shard_map/while/body/dynamic_update_slice | solution.py:100
  361.6 11.7 %dynamic_update_slice.4 = f32[2,2,512,384]{3,2,1,0:T(8,128)} dynamic-update-slice(f32[2,2,512,384]{3,2,1,0:T(8,128)} %get-tuple-element.186, f32[2,2,256,256]{3,2,1,0:T(8,128)S(1)} %bitcast_add_fusion.2, s32[]{:T(128)} %constant.72.clone.1..sunk, s32[]{:T(128)} %constant.72.clone.1..sunk, s32[]{:T(128)S(6)} %select_n.288, s32[]{:T(128)S(6)} %select_n.289) | dynamic-update-slice | bytes 2097156 | tf_op jit(solution)/shard_map/while/body/dynamic_update_slice | solution.py:100
  380.4 11.6 %dynamic_update_slice.4 = f32[2,2,512,384]{3,2,1,0:T(8,128)} dynamic-update-slice(f32[2,2,512,384]{3,2,1,0:T(8,128)} %get-tuple-element.186, f32[2,2,256,256]{3,2,1,0:T(8,128)S(1)} %bitcast_add_fusion.2, s32[]{:T(128)} %constant.72.clone.1..sunk, s32[]{:T(128)} %constant.72.clone.1..sunk, s32[]{:T(128)S(6)} %select_n.288, s32[]{:T(128)S(6)} %select_n.289) | dynamic-update-slice | bytes 2097156 | tf_op jit(solution)/shard_map/while/body/dynamic_update_slice | solution.py:100
  399.1 11.3 %dynamic_update_slice.4 = f32[2,2,512,384]{3,2,1,0:T(8,128)} dynamic-update-slice(f32[2,2,512,384]{3,2,1,0:T(8,128)} %get-tuple-element.186, f32[2,2,256,256]{3,2,1,0:T(8,128)S(1)} %bitcast_add_fusion.2, s32[]{:T(128)} %constant.72.clone.1..sunk, s32[]{:T(128)} %constant.72.clone.1..sunk, s32[]{:T(128)S(6)} %select_n.288, s32[]{:T(128)S(6)} %select_n.289) | dynamic-update-slice | bytes 2097156 | tf_op jit(solution)/shard_map/while/body/dynamic_update_slice | solution.py:100
  410.5 120.5 %all-reduce.6.cloned.1.call-done = f32[2,2,512,384]{3,2,1,0:T(8,128)} async-done(((f32[2,2,512,384]{3,2,1,0:T(8,128)}), f32[2,2,512,384]{3,2,1,0:T(8,128)}) %all-reduce.6.cloned.1.call-update) | async-done | bytes 3145744 | tf_op jit(solution)/shard_map/psum | solution.py:122
  530.9 2.8 slice.80
  533.7 2.7 collective-permute-start.1
  537.8 62.4 %all-reduce.8.cloned.1.call-done = f32[2,2,256,256]{3,2,0,1:T(8,128)} async-done(((f32[2,2,256,256]{3,2,0,1:T(8,128)}), f32[2,2,256,256]{3,2,0,1:T(8,128)}) %all-reduce.8.cloned.1.call-update) | async-done | bytes 1048592 | tf_op jit(solution)/shard_map/psum | solution.py:125
  602.5 2.7 slice_add_fusion
  (88 shorter events, 38.2 us)
Async XLA Ops:
  7.2 206.1 %all-reduce.4.cloned.1.call-start = ((), (), s32[]{:S(2)}) async-start(), calls=%async_computation | async-start | bytes 2097152 | tf_op jit(solution)/shard_map/psum | solution.py:108
  7.2 7.8 %collective-permute-start = (f32[2,2,256,384]{3,2,1,0:T(8,128)}, f32[2,2,256,384]{3,2,1,0:T(8,128)}, u32[]{:S(2)}, u32[]{:S(2)}) collective-permute-start(f32[2,2,256,384]{3,2,1,0:T(8,128)} %param.13), channel_id=1, source_target_pairs={{4,0},{8,4},{12,8},{16,12},{20,16},{24,20},{28,24},{5,1},{9,5},{13... | collective-permute-start | bytes 4718600 | tf_op jit(solution)/shard_map/ppermute | solution.py:14
  10.0 5.0 copy-start.17
  29.2 2.7 copy-start.10
  29.2 2.7 copy-start.12
  31.9 22.2 %copy-start.4 = (f32[4,256,256]{2,1,0:T(8,128)}, f32[4,256,256]{2,1,0:T(8,128)S(1)}, u32[]{:S(2)}) copy-start(f32[4,256,256]{2,1,0:T(8,128)S(1)} %get-tuple-element.90) | copy-start | bytes 3145732
  63.2 4.9 copy-start.8
  100.3 27.9 %copy-start = (f32[4,2,256,256]{3,2,1,0:T(8,128)}, f32[4,2,256,256]{3,2,1,0:T(8,128)S(1)}, u32[]{:S(2)}) copy-start(f32[4,2,256,256]{3,2,1,0:T(8,128)S(1)} %fusion.70) | copy-start | bytes 6291460
  104.8 23.4 %copy-start.2 = (f32[4,2,256,256]{3,2,1,0:T(8,128)}, f32[4,2,256,256]{3,2,1,0:T(8,128)S(1)}, u32[]{:S(2)}) copy-start(f32[4,2,256,256]{3,2,1,0:T(8,128)S(1)} %fusion.73) | copy-start | bytes 6291460
  137.6 7.2 %copy-start.6 = (f32[4,2,256,256]{3,2,1,0:T(8,128)}, f32[4,2,256,256]{3,2,1,0:T(8,128)S(1)}, u32[]{:S(2)}) copy-start(f32[4,2,256,256]{3,2,1,0:T(8,128)S(1)} %multiply_subtract_fusion.4) | copy-start | bytes 6291460
  144.8 386.1 %all-reduce.6.cloned.1.call-start = ((), (), s32[]{:S(2)}) async-start(), calls=%async_computation.1 | async-start | bytes 6291456 | tf_op jit(solution)/shard_map/psum | solution.py:122
  213.3 2.2 copy-start.14
  220.0 4.5 copy-start.7
  243.1 4.5 copy-start.1
  243.1 4.5 copy-start.3
  285.8 4.6 copy-start.9
  318.7 4.5 copy-start.5
  318.7 4.5 copy-start.11
  318.7 4.5 copy-start.13
  333.4 1.9 copy-start.18
  333.4 1.9 copy-start.19
  410.4 189.7 %all-reduce.8.cloned.1.call-start = ((), (), s32[]{:S(2)}) async-start(), calls=%async_computation.2 | async-start | bytes 2097152 | tf_op jit(solution)/shard_map/psum | solution.py:125
  530.9 5.5 copy-start.15
  533.7 68.7 %collective-permute-start.1 = (f32[2,2,256,384]{3,2,1,0:T(8,128)}, f32[2,2,256,384]{3,2,1,0:T(8,128)}, u32[]{:S(2)}, u32[]{:S(2)}) collective-permute-start(f32[2,2,256,384]{3,2,1,0:T(8,128)} %slice.80), channel_id=1, source_target_pairs={{0,4},{4,8},{8,12},{12,16},{16,20},{20,24},{24,28},{1,5},{5,9},{9,... | collective-permute-start | bytes 4718600 | tf_op jit(solution)/shard_map/ppermute | solution.py:14
  537.7 64.7 %copy-start.16 = (f32[2,2,512,384]{3,2,1,0:T(8,128)S(1)}, f32[2,2,512,384]{3,2,1,0:T(8,128)}, u32[]{:S(2)}) copy-start(f32[2,2,512,384]{3,2,1,0:T(8,128)} %all-reduce.6.cloned.1.call-done) | copy-start | bytes 9437188
Sparse Core Ops, SparseCore 0:
  144.9 68.2 all-reduce.3
  410.6 120.3 all-reduce.5
  537.9 62.2 all-reduce.7
where the time goes:
time: 624 us; the launch traced here: 612 us
  waiting for transfers between devices  250 us (40%)
  matrix products  228 us (37%)
  local copies, waits for them, and re-layouts  78.8 us (13%)
  other arithmetic  19.9 us (3%)
  loops' own time  15.6 us (2%)
  between operations  15.4 us (2%)
    psum x1, waiting for transfers between devices, per_device(): summed = lax.psum(grad_ext, 'mode')  120 us
    dot_general x24, matrix products, on_right(): return jnp.einsum('mjk,kl->mjl', field, matrix, precision=HIGH)  115 us
    dot_general x24, matrix products, on_left(): return jnp.einsum('jk,mkl->mjl', matrix, field, precision=HIGH)  113 us
    psum x1, waiting for transfers between devices, per_device(): power = lax.psum(local_power, 'mode')  67.4 us
    psum x1, waiting for transfers between devices, per_device(): probe_grad = lax.psum(grad_probe, 'tile')  62.4 us
    dynamic_update_slice x4, local copies, waits for them, and re-layouts, place_terms(): return lax.dynamic_update_slice(grad_ext, current + pieces, start)  46.5 us
    another operation x1, loops' own time, per_device(): lax.fori_loop(zero_index, jnp.full((), slot_total, jnp.int32), add_slot,...  15.6 us
    gather x12, local copies, waits for them, and re-layouts  12.5 us
  transfers between devices with their start and end apart: 5, of which 3 were waited for; matrix products, arithmetic and copies ran while one was open for 2% of the time, Pallas kernels for 0%

commit v1 on v0

--- a/solution.py
+++ b/solution.py
@@ -3,6 +3,7 @@
 import jax.numpy as jnp
 from jax import lax
 from jax.sharding import PartitionSpec as P
+from jax.lax import all_gather
 
 MODES = 8
 HIGH = lax.Precision.HIGHEST
@@ -105,7 +106,7 @@
         windows
     )
     local_power = jnp.sum(far_field[0] * far_field[0] + far_field[1] * far_field[1], axis=1)
-    power = lax.psum(local_power, "mode")
+    power = jnp.sum(all_gather(local_power, "mode"), axis=0)
     alive = (jnp.arange(slot_total, dtype=jnp.int32) < live_count).astype(jnp.float32)
     weight = (power - measured) / MODES * alive[:, None, None]
 

time: 624 us -> 655 us (1.050)
  waiting for transfers between devices: 250 us -> 278 us
    all_gather x0 -> x1, waiting for transfers between devices: none -> 96.1 us  [per_device(): power = jnp.sum(all_gather(local_power, 'mode'), axis=0)]
    psum x1 -> x0, waiting for transfers between devices: 67.4 us -> none  [per_device(): power = lax.psum(local_power, 'mode')]
where the time goes in v1:
time: 655 us; the launch traced here: 644 us
  waiting for transfers between devices  278 us (42%)
  matrix products  228 us (35%)
  local copies, waits for them, and re-layouts  78.9 us (12%)
  other arithmetic  23.5 us (4%)
  loops' own time  15.6 us (2%)
  between operations  15.5 us (2%)
    psum x1, waiting for transfers between devices, per_device(): summed = lax.psum(grad_ext, 'mode')  120 us
    dot_general x24, matrix products, on_right(): return jnp.einsum('mjk,kl->mjl', field, matrix, precision=HIGH)  115 us
    dot_general x24, matrix products, on_left(): return jnp.einsum('jk,mkl->mjl', matrix, field, precision=HIGH)  112 us
    all_gather x1, waiting for transfers between devices, per_device(): power = jnp.sum(all_gather(local_power, 'mode'), axis=0)  96.1 us
    psum x1, waiting for transfers between devices, per_device(): probe_grad = lax.psum(grad_probe, 'tile')  62.4 us
    dynamic_update_slice x4, local copies, waits for them, and re-layouts, place_terms(): return lax.dynamic_update_slice(grad_ext, current + pieces, start)  46.5 us
    another operation x1, loops' own time, per_device(): lax.fori_loop(zero_index, jnp.full((), slot_total, jnp.int32), add_slot,...  15.6 us
  transfers between devices with their start and end apart: 5, of which 3 were waited for; matrix products, arithmetic and copies ran while one was open for 2% of the time, Pallas kernels for 0%

profile of v1, /device:TPU:0, one launch (start us, length us, event | category | flops | bytes accessed | tf_op | source)
XLA Modules:
  0.0 643.8 jit_solution(3595766616273387384)
XLA Ops:
  10.1 2.6 fusion.421
  16.7 12.5 %while.14 = (s32[]{:T(128)}, f32[2,2,512,384]{3,2,1,0:T(8,128)S(1)}, s32[4,4]{1,0:T(4,128)S(1)}, f32[4,2,2,256,256]{4,3,2,1,0:T(8,128)}, s32[]{:T(128)}) while((s32[]{:T(128)}, f32[2,2,512,384]{3,2,1,0:T(8,128)S(1)}, s32[4,4]{1,0:T(4,128)S(1)}, f32[4,2,2,256,256]{4,3,2,1,0:T(8,128)}, s32[]{:T(128)}) %tuple.57), condition=%wide.while_cond.1, body=%wide.while_body.1.sunk | while | flops 2 | bytes 2098801 | solution.py:96
  20.4 2.5 bitcast_dynamic-update-slice_fusion.2
  29.2 2.7 slice_bitcast_fusion.3
  32.0 4.5 fusion.49
  36.5 4.4 fusion.48
  40.9 4.6 multiply_add_fusion.9
  45.5 4.3 fusion.40
  49.8 4.3 fusion.42
  54.2 4.7 multiply_subtract_fusion.9
  58.8 4.5 multiply_add_fusion.8
  63.3 4.8 multiply_subtract_fusion.8
  68.2 4.6 fusion.116
  72.8 4.6 fusion.117
  77.4 4.8 convolution_add_fusion.1
  82.2 4.5 fusion.34
  86.6 4.5 fusion.32
  91.1 4.8 convolution_subtract_fusion.1
  95.9 4.5 fusion.70
  100.4 4.5 fusion.73
  104.9 5.0 fusion.165
  109.9 4.6 fusion.162
  114.6 4.8 multiply_add_fusion.5
  119.4 4.5 fusion.26
  123.8 4.5 fusion.24
  128.3 4.8 multiply_subtract_fusion.5
  133.2 4.5 multiply_subtract_fusion.4
  137.7 7.2 %add_reduce_fusion.2 = (f32[4,256,256]{2,1,0:T(8,128)}, f32[4,2,256,256]{3,2,1,0:T(8,128)}) fusion(f32[4,2,256,256]{3,2,1,0:T(8,128)S(1)} %multiply_subtract_fusion.4, f32[4,2,256,256]{3,2,1,0:T(8,128)S(1)} %fusion.24, f32[4,2,256,256]{3,2,1,0:T(8,128)S(1)} %multiply_subtract_fusion.5), kind=kOutput, calls=%fused_computation.70 | convolution fusion | flops 1614479360 | bytes 9437184 | tf_op jit(solution)/shard_map/vmap(mjk,kl->mjl)/dot_general | solution.py:31
  146.0 96.1 %all-gather.3.cloned.1.call-done = f32[16,256,256]{2,1,0:T(8,128)} async-done(((f32[4,256,256]{2,1,0:T(8,128)}), f32[16,256,256]{2,1,0:T(8,128)}) %all-gather.3.cloned.1.call-update) | async-done | bytes 4194320 | tf_op jit(solution)/shard_map/all_gather | solution.py:109
  242.1 3.6 reduce_sum.64
  247.9 4.5 fusion.54
  252.4 4.5 fusion.52
  256.9 4.7 fusion.63
  261.6 4.6 fusion.18
  266.2 4.6 fusion.16
  270.7 4.7 fusion.60
  275.5 4.5 fusion.80
  280.0 5.6 add_reduce_fusion
  285.6 4.6 fusion.155
  290.2 4.6 fusion.152
  294.9 4.8 multiply_add_fusion.2
  299.7 4.5 fusion.8
  304.2 4.5 fusion.10
  308.7 4.9 multiply_subtract_fusion.2
  313.6 4.6 multiply_add_fusion.1
  318.2 5.0 multiply_subtract_fusion.1
  323.2 4.6 fusion.118
  327.8 4.6 fusion.119
  332.4 4.8 convolution_add_fusion
  337.2 4.5 fusion.2
  341.7 4.5 fusion
  346.2 4.9 convolution_subtract_fusion
  351.1 4.5 fusion.90
  355.6 7.6 %add_bitcast_fusion = (f32[4,2,1,256,256]{4,3,1,0,2:T(8,128)S(1)}, f32[4,2,1,256,256]{4,3,1,0,2:T(8,128)}, f32[4,256,256]{2,1,0:T(8,128)S(1)}, f32[4,256,256]{2,1,0:T(8,128)S(1)}) fusion(f32[4,2,256,256]{3,2,1,0:T(8,128)S(1)} %fusion.90, f32[4,256,256]{2,1,0:T(8,128)S(1)} %get-tuple-element.89, f32[4,256,256]{2,1,0:T(8,128)S(1)} %copy-done.5, ...), kind=kOutput, calls=%fused_computation.57 | convolution fusion | flops 1618935808 | bytes 15728640 | tf_op jit(solution)/shard_map/vmap(mjk,kl->mjl)/dot_general | solution.py:31
  367.7 75.1 %while.13 = (s32[]{:T(128)}, f32[2,2,512,384]{3,2,1,0:T(8,128)}, s32[4]{0:T(128)S(1)}, s32[4]{0:T(128)S(1)}, f32[4,2,2,256,256]{4,3,2,1,0:T(8,128)}, /*index=5*/s32[]{:T(128)}, s32[]{:T(128)}, s32[]{:T(128)}, s32[]{:T(128)}) while((s32[]{:T(128)}, f32[2,2,512,384]{3,2,1,0:T(8,128)}, s32[4]{0:T(128)S(1)}, s32[4]{0:T(128)S(1)}, ...), condition=%wide.region_7.8_spmd, body=%wide.region_6.7_spmd.sunk | while | flops 262152 | bytes 5243081 | solution.py:122
  374.8 11.9 %dynamic_update_slice.4 = f32[2,2,512,384]{3,2,1,0:T(8,128)} dynamic-update-slice(f32[2,2,512,384]{3,2,1,0:T(8,128)} %get-tuple-element.186, f32[2,2,256,256]{3,2,1,0:T(8,128)S(1)} %bitcast_add_fusion.2, s32[]{:T(128)} %constant.72.clone.1..sunk, s32[]{:T(128)} %constant.72.clone.1..sunk, s32[]{:T(128)S(6)} %select_n.288, s32[]{:T(128)S(6)} %select_n.289) | dynamic-update-slice | bytes 2097156 | tf_op jit(solution)/shard_map/while/body/dynamic_update_slice | solution.py:101
  394.0 11.7 %dynamic_update_slice.4 = f32[2,2,512,384]{3,2,1,0:T(8,128)} dynamic-update-slice(f32[2,2,512,384]{3,2,1,0:T(8,128)} %get-tuple-element.186, f32[2,2,256,256]{3,2,1,0:T(8,128)S(1)} %bitcast_add_fusion.2, s32[]{:T(128)} %constant.72.clone.1..sunk, s32[]{:T(128)} %constant.72.clone.1..sunk, s32[]{:T(128)S(6)} %select_n.288, s32[]{:T(128)S(6)} %select_n.289) | dynamic-update-slice | bytes 2097156 | tf_op jit(solution)/shard_map/while/body/dynamic_update_slice | solution.py:101
  412.8 11.6 %dynamic_update_slice.4 = f32[2,2,512,384]{3,2,1,0:T(8,128)} dynamic-update-slice(f32[2,2,512,384]{3,2,1,0:T(8,128)} %get-tuple-element.186, f32[2,2,256,256]{3,2,1,0:T(8,128)S(1)} %bitcast_add_fusion.2, s32[]{:T(128)} %constant.72.clone.1..sunk, s32[]{:T(128)} %constant.72.clone.1..sunk, s32[]{:T(128)S(6)} %select_n.288, s32[]{:T(128)S(6)} %select_n.289) | dynamic-update-slice | bytes 2097156 | tf_op jit(solution)/shard_map/while/body/dynamic_update_slice | solution.py:101
  431.5 11.3 %dynamic_update_slice.4 = f32[2,2,512,384]{3,2,1,0:T(8,128)} dynamic-update-slice(f32[2,2,512,384]{3,2,1,0:T(8,128)} %get-tuple-element.186, f32[2,2,256,256]{3,2,1,0:T(8,128)S(1)} %bitcast_add_fusion.2, s32[]{:T(128)} %constant.72.clone.1..sunk, s32[]{:T(128)} %constant.72.clone.1..sunk, s32[]{:T(128)S(6)} %select_n.288, s32[]{:T(128)S(6)} %select_n.289) | dynamic-update-slice | bytes 2097156 | tf_op jit(solution)/shard_map/while/body/dynamic_update_slice | solution.py:101
  442.9 119.7 %all-reduce.3.cloned.1.call-done = f32[2,2,512,384]{3,2,1,0:T(8,128)} async-done(((f32[2,2,512,384]{3,2,1,0:T(8,128)}), f32[2,2,512,384]{3,2,1,0:T(8,128)}) %all-reduce.3.cloned.1.call-update) | async-done | bytes 3145744 | tf_op jit(solution)/shard_map/psum | solution.py:123
  562.6 2.8 slice.80
  565.4 2.7 collective-permute-start.1
  569.4 62.4 %all-reduce.5.cloned.1.call-done = f32[2,2,256,256]{3,2,0,1:T(8,128)} async-done(((f32[2,2,256,256]{3,2,0,1:T(8,128)}), f32[2,2,256,256]{3,2,0,1:T(8,128)}) %all-reduce.5.cloned.1.call-update) | async-done | bytes 1048592 | tf_op jit(solution)/shard_map/psum | solution.py:126
  634.1 2.7 slice_add_fusion
  (89 shorter events, 40.8 us)
Async XLA Ops:
  7.2 234.9 %all-gather.3.cloned.1.call-start = ((), (), s32[]{:S(2)}) async-start(), calls=%async_computation.2 | async-start | bytes 5242880 | tf_op jit(solution)/shard_map/all_gather | solution.py:109
  7.2 7.9 %collective-permute-start = (f32[2,2,256,384]{3,2,1,0:T(8,128)}, f32[2,2,256,384]{3,2,1,0:T(8,128)}, u32[]{:S(2)}, u32[]{:S(2)}) collective-permute-start(f32[2,2,256,384]{3,2,1,0:T(8,128)} %param.13), channel_id=1, source_target_pairs={{4,0},{8,4},{12,8},{16,12},{20,16},{24,20},{28,24},{5,1},{9,5},{13... | collective-permute-start | bytes 4718600 | tf_op jit(solution)/shard_map/ppermute | solution.py:15
  10.0 5.0 copy-start.17
  29.2 2.7 copy-start.10
  29.2 2.7 copy-start.12
  31.9 22.2 %copy-start.4 = (f32[4,256,256]{2,1,0:T(8,128)}, f32[4,256,256]{2,1,0:T(8,128)S(1)}, u32[]{:S(2)}) copy-start(f32[4,256,256]{2,1,0:T(8,128)S(1)} %get-tuple-element.90) | copy-start | bytes 3145732
  63.3 4.9 copy-start.8
  100.4 27.9 %copy-start = (f32[4,2,256,256]{3,2,1,0:T(8,128)}, f32[4,2,256,256]{3,2,1,0:T(8,128)S(1)}, u32[]{:S(2)}) copy-start(f32[4,2,256,256]{3,2,1,0:T(8,128)S(1)} %fusion.70) | copy-start | bytes 6291460
  104.9 23.4 %copy-start.2 = (f32[4,2,256,256]{3,2,1,0:T(8,128)}, f32[4,2,256,256]{3,2,1,0:T(8,128)S(1)}, u32[]{:S(2)}) copy-start(f32[4,2,256,256]{3,2,1,0:T(8,128)S(1)} %fusion.73) | copy-start | bytes 6291460
  137.7 7.2 %copy-start.6 = (f32[4,2,256,256]{3,2,1,0:T(8,128)}, f32[4,2,256,256]{3,2,1,0:T(8,128)S(1)}, u32[]{:S(2)}) copy-start(f32[4,2,256,256]{3,2,1,0:T(8,128)S(1)} %multiply_subtract_fusion.4) | copy-start | bytes 6291460
  144.9 417.7 %all-reduce.3.cloned.1.call-start = ((), (), s32[]{:S(2)}) async-start(), calls=%async_computation | async-start | bytes 6291456 | tf_op jit(solution)/shard_map/psum | solution.py:123
  245.7 2.2 copy-start.14
  252.4 4.5 copy-start.7
  275.5 4.5 copy-start.1
  275.5 4.5 copy-start.3
  318.2 5.0 copy-start.9
  351.1 4.5 copy-start.5
  351.1 4.5 copy-start.11
  351.1 4.5 copy-start.13
  365.8 1.9 copy-start.18
  365.8 1.9 copy-start.19
  442.8 189.0 %all-reduce.5.cloned.1.call-start = ((), (), s32[]{:S(2)}) async-start(), calls=%async_computation.1 | async-start | bytes 2097152 | tf_op jit(solution)/shard_map/psum | solution.py:126
  562.6 5.5 copy-start.15
  565.4 68.7 %collective-permute-start.1 = (f32[2,2,256,384]{3,2,1,0:T(8,128)}, f32[2,2,256,384]{3,2,1,0:T(8,128)}, u32[]{:S(2)}, u32[]{:S(2)}) collective-permute-start(f32[2,2,256,384]{3,2,1,0:T(8,128)} %slice.80), channel_id=1, source_target_pairs={{0,4},{4,8},{8,12},{12,16},{16,20},{20,24},{24,28},{1,5},{5,9},{9,... | collective-permute-start | bytes 4718600 | tf_op jit(solution)/shard_map/ppermute | solution.py:15
  569.4 64.7 %copy-start.16 = (f32[2,2,512,384]{3,2,1,0:T(8,128)S(1)}, f32[2,2,512,384]{3,2,1,0:T(8,128)}, u32[]{:S(2)}) copy-start(f32[2,2,512,384]{3,2,1,0:T(8,128)} %all-reduce.3.cloned.1.call-done) | copy-start | bytes 9437188
Sparse Core Ops, SparseCore 0:
  145.0 97.0 all-gather.2
  443.0 119.5 all-reduce.2
  569.5 62.2 all-reduce.4
